TPU v7x, 256 devices: a whole 4x4x8 slice. The times are simulated.
256 devices in a mesh: req: 4 (over z_hi, core), ctx: 64 (over x, y, z_lo).
Axes of the slice: x: 4, y: 4, z: 8 (z_hi: 2, z_lo: 4; z = z_hi * 4 + z_lo), core: 2. Of those that a mesh axis runs over, the one named last changes fastest.
Arguments:
- query_rows: bfloat16 [4, 7168, 2048], P('req', 'ctx'), may hold values from -120 to 120
- key_rows: bfloat16 [4, 7168, 1024], P('req', 'ctx'), may hold values from -8 to 8
- value_rows: bfloat16 [4, 7168, 1024], P('req', 'ctx'), may hold values from -6 to 6
- image_starts: int32 [4, 14], P('req'), may hold values from 0 to 6912, as said below
- image_counts: int32 [4], P('req'), may hold values from 1 to 14, as said below
Outputs:
- attended: bfloat16 [4, 7168, 2048], P('req', 'ctx')
Inputs may be any that keep to these rules, and one draw needn't show every extreme that they name: `image_starts`: each request's row holds 14 distinct multiples of 256 in ascending order, always starting with 0; in some request the last entry is (27) * 256; only the first image_counts entries of a request are image blocks. `image_counts`: some request has 14 image blocks.
All inputs are finite; a program needn't handle non-finite values.
Results may differ from a plain program's by a relative error of at most 0.0059.
Values may be sent and summed in bfloat16 or wider, within the bound.
A program may use at most 128 MiB of HBM per device.

v0:
```python
import jax
import jax.numpy as jnp
from jax import lax
from jax.sharding import PartitionSpec as P

HEADS = 16
KV_HEADS = 8
HEAD_DIM = 128
IMG = 256
score_scale = 168.0 ** (-0.5)


def image_ids(position, starts, count):
    index = jnp.arange(starts.shape[0], dtype=jnp.int32)
    inside = (
        (starts[None, :] <= position[:, None])
        & (position[:, None] < starts[None, :] + IMG)
        & (index[None, :] < count)
    )
    return jnp.sum(jnp.where(inside, index[None, :] + 1, 0), axis=1) - 1


def shards(query_rows, key_rows, value_rows, image_starts, image_counts):
    my_index = lax.axis_index("ctx")
    row_count = query_rows.shape[1]
    starts = image_starts[0]
    count = image_counts[0]
    local_pos = jnp.arange(row_count, dtype=jnp.int32)
    query_pos = my_index * row_count + local_pos
    query_ids = image_ids(query_pos, starts, count)
    group = HEADS // KV_HEADS
    query_heads = query_rows[0].reshape(row_count, KV_HEADS, group, HEAD_DIM)
    initial = (
        jnp.full((KV_HEADS, group, row_count), -1e30, jnp.float32),
        jnp.zeros((KV_HEADS, group, row_count), jnp.float32),
        jnp.zeros((KV_HEADS, group, row_count, HEAD_DIM), jnp.float32),
    )

    def add_block(state, key_block, value_block, key_pos):
        key_ids = image_ids(key_pos, starts, count)
        visible = (key_pos[None, :] <= query_pos[:, None]) | (
            key_ids[None, :] == query_ids[:, None]
        ) & (query_ids[:, None] >= 0)

        def update(carried):
            running_max, running_total, running_sum = carried
            scores = (
                jnp.einsum(
                    "qkgd,skd->kgqs", query_heads, key_block, preferred_element_type=jnp.float32
                )
                * score_scale
            )
            scores = jnp.where(visible[None, None], scores, -1e30)
            new_max = jnp.maximum(running_max, jnp.max(scores, axis=-1))
            factor = jnp.exp(running_max - new_max)
            weights = jnp.where(visible[None, None], jnp.exp(scores - new_max[..., None]), 0.0)
            new_total = running_total * factor + jnp.sum(weights, axis=-1)
            product = jnp.einsum(
                "kgqs,skd->kgqd",
                weights.astype(jnp.bfloat16),
                value_block,
                preferred_element_type=jnp.float32,
            )
            return (new_max, new_total, running_sum * factor[..., None] + product)

        return lax.cond(jnp.any(visible), update, lambda carried: carried, state)

    start = jnp.int32(0)
    key_piece = lax.all_gather(key_rows, "ctx", axis=1, tiled=True)
    value_piece = lax.all_gather(value_rows, "ctx", axis=1, tiled=True)
    piece_rows = key_piece.shape[1]
    block_rows = max(
        (size for size in range(1, min(piece_rows, 1024) + 1) if piece_rows % size == 0)
    )
    block_total = piece_rows // block_rows
    key_blocks = key_piece[0].reshape(block_total, block_rows, KV_HEADS, HEAD_DIM)
    value_blocks = value_piece[0].reshape(block_total, block_rows, KV_HEADS, HEAD_DIM)

    def scan_step(carried, items):
        key_block, value_block, block_index = items
        key_pos = start + block_index * block_rows + jnp.arange(block_rows, dtype=jnp.int32)
        return (add_block(carried, key_block, value_block, key_pos), None)

    result, unused = lax.scan(
        scan_step, initial, (key_blocks, value_blocks, jnp.arange(block_total, dtype=jnp.int32))
    )
    final_max, final_total, final_sum = result
    output = final_sum / final_total[..., None]
    output = output.transpose(2, 0, 1, 3).reshape(row_count, HEADS * HEAD_DIM).astype(jnp.bfloat16)
    return output[None]


def solution(mesh):
    return jax.shard_map(
        shards,
        mesh=mesh,
        in_specs=(
            P("req", "ctx", None),
            P("req", "ctx", None),
            P("req", "ctx", None),
            P("req", None),
            P("req"),
        ),
        out_specs=P("req", "ctx", None),
        check_vma=False,
    )
```

profile of v0, /device:TPU:126, one launch (start us, length us, event | category | flops | bytes accessed | tf_op | source)
XLA Modules:
  0.0 935.1 jit_solution(16546968612578805428)
XLA Ops:
  6.5 0.7 all-gather.3.cloned.1.call-update
  7.3 0.7 all-gather.5.cloned.1.call-update
  8.7 1.3 reshape_squeeze.10
  10.2 0.7 add_bitcast_fusion
  10.8 0.7 select_reduce_fusion.1
  11.6 402.7 %all-gather.3.cloned.1.call-done = bf16[1,7168,1024]{2,1,0:T(8,128)(2,1)} async-done(((bf16[1,112,1024]{2,1,0:T(8,128)(2,1)}), bf16[1,7168,1024]{2,1,0:T(8,128)(2,1)}) %all-gather.3.cloned.1.call-update) | async-done | bytes 14680080 | tf_op jit(solution)/shard_map/all_gather | solution.py:69
  414.3 9.1 copy.17
  423.5 6.5 copy.11
  430.0 388.6 %all-gather.5.cloned.1.call-done = bf16[1,7168,1024]{2,1,0:T(8,128)(2,1)} async-done(((bf16[1,112,1024]{2,1,0:T(8,128)(2,1)}), bf16[1,7168,1024]{2,1,0:T(8,128)(2,1)}) %all-gather.5.cloned.1.call-update) | async-done | bytes 14680080 | tf_op jit(solution)/shard_map/all_gather | solution.py:70
  818.6 9.1 copy.18
  827.7 6.4 copy.13
  834.2 92.3 %while.17 = (s32[]{:T(128)}, f32[8,2,112]{2,1,0:T(2,128)S(1)}, f32[8,2,112]{2,1,0:T(2,128)S(1)}, f32[8,2,112,128]{3,2,1,0:T(8,128)S(1)}, s32[7]{0:T(128)S(1)}, /...) while((s32[]{:T(128)}, f32[8,2,112]{2,1,0:T(2,128)S(1)}, ...), condition=%wide.region_8.9_spmd.clone, body=%wide.region_1.8_spmd.clone.sunk | while | flops 964502272 | bytes 29113972 | solution.py:84
  834.2 0.7 dynamic_slice.40
  835.6 0.7 iota_compare_fusion.3
  836.4 0.9 fusion.27
  838.0 9.4 %conditional.3 = ((f32[8,2,112]{2,1,0:T(2,128)S(1)}, f32[8,2,112]{2,1,0:T(2,128)S(1)}, f32[8,2,112,128]{3,2,1,0:T(8,128)S(1)})) conditional(s32[]{:T(128)} %convert_element_type.39, (f32[8,2,112]{2,1,0:T(2,128)S(1)}, f32[8,2,112]{2,1,0:T(2,128)S(1)}, f32[8,2,112,128]{3,2,1,0:T(8,128)S(1)}) %tuple.57, (pred[112,1024]{1,0:T(8,128)(4,1)S(1)}, ...), branch_computations={%region_4.4_spmd, %region_5.7_spmd} | conditional | flops 963841536 | bytes 28967968 | solution.py:66
  838.0 3.0 fusion.2
  841.1 2.4 fusion.4
  843.5 3.9 fusion.13
  847.4 0.7 dynamic_slice.40
  848.8 0.7 iota_compare_fusion.3
  849.6 0.9 fusion.27
  851.2 9.4 %conditional.3 = ((f32[8,2,112]{2,1,0:T(2,128)S(1)}, f32[8,2,112]{2,1,0:T(2,128)S(1)}, f32[8,2,112,128]{3,2,1,0:T(8,128)S(1)})) conditional(s32[]{:T(128)} %convert_element_type.39, (f32[8,2,112]{2,1,0:T(2,128)S(1)}, f32[8,2,112]{2,1,0:T(2,128)S(1)}, f32[8,2,112,128]{3,2,1,0:T(8,128)S(1)}) %tuple.57, (pred[112,1024]{1,0:T(8,128)(4,1)S(1)}, ...), branch_computations={%region_4.4_spmd, %region_5.7_spmd} | conditional | flops 963841536 | bytes 28967968 | solution.py:66
  851.2 3.0 fusion.2
  854.3 2.4 fusion.4
  856.7 3.9 fusion.13
  860.6 0.7 dynamic_slice.40
  862.0 0.7 iota_compare_fusion.3
  862.8 0.9 fusion.27
  864.4 9.4 %conditional.3 = ((f32[8,2,112]{2,1,0:T(2,128)S(1)}, f32[8,2,112]{2,1,0:T(2,128)S(1)}, f32[8,2,112,128]{3,2,1,0:T(8,128)S(1)})) conditional(s32[]{:T(128)} %convert_element_type.39, (f32[8,2,112]{2,1,0:T(2,128)S(1)}, f32[8,2,112]{2,1,0:T(2,128)S(1)}, f32[8,2,112,128]{3,2,1,0:T(8,128)S(1)}) %tuple.57, (pred[112,1024]{1,0:T(8,128)(4,1)S(1)}, ...), branch_computations={%region_4.4_spmd, %region_5.7_spmd} | conditional | flops 963841536 | bytes 28967968 | solution.py:66
  864.4 3.0 fusion.2
  867.4 2.4 fusion.4
  869.8 3.9 fusion.13
  873.8 0.7 dynamic_slice.40
  875.1 0.7 iota_compare_fusion.3
  875.9 0.9 fusion.27
  877.6 9.4 %conditional.3 = ((f32[8,2,112]{2,1,0:T(2,128)S(1)}, f32[8,2,112]{2,1,0:T(2,128)S(1)}, f32[8,2,112,128]{3,2,1,0:T(8,128)S(1)})) conditional(s32[]{:T(128)} %convert_element_type.39, (f32[8,2,112]{2,1,0:T(2,128)S(1)}, f32[8,2,112]{2,1,0:T(2,128)S(1)}, f32[8,2,112,128]{3,2,1,0:T(8,128)S(1)}) %tuple.57, (pred[112,1024]{1,0:T(8,128)(4,1)S(1)}, ...), branch_computations={%region_4.4_spmd, %region_5.7_spmd} | conditional | flops 963841536 | bytes 28967968 | solution.py:66
  877.6 3.0 fusion.2
  880.6 2.4 fusion.4
  883.0 3.9 fusion.13
  887.0 0.7 dynamic_slice.40
  888.3 0.7 iota_compare_fusion.3
  889.1 0.9 fusion.27
  890.7 9.4 %conditional.3 = ((f32[8,2,112]{2,1,0:T(2,128)S(1)}, f32[8,2,112]{2,1,0:T(2,128)S(1)}, f32[8,2,112,128]{3,2,1,0:T(8,128)S(1)})) conditional(s32[]{:T(128)} %convert_element_type.39, (f32[8,2,112]{2,1,0:T(2,128)S(1)}, f32[8,2,112]{2,1,0:T(2,128)S(1)}, f32[8,2,112,128]{3,2,1,0:T(8,128)S(1)}) %tuple.57, (pred[112,1024]{1,0:T(8,128)(4,1)S(1)}, ...), branch_computations={%region_4.4_spmd, %region_5.7_spmd} | conditional | flops 963841536 | bytes 28967968 | solution.py:66
  890.8 3.0 fusion.2
  893.8 2.4 fusion.4
  896.2 3.9 fusion.13
  900.1 0.7 dynamic_slice.40
  901.5 0.7 iota_compare_fusion.3
  902.3 0.9 fusion.27
  903.9 9.4 %conditional.3 = ((f32[8,2,112]{2,1,0:T(2,128)S(1)}, f32[8,2,112]{2,1,0:T(2,128)S(1)}, f32[8,2,112,128]{3,2,1,0:T(8,128)S(1)})) conditional(s32[]{:T(128)} %convert_element_type.39, (f32[8,2,112]{2,1,0:T(2,128)S(1)}, f32[8,2,112]{2,1,0:T(2,128)S(1)}, f32[8,2,112,128]{3,2,1,0:T(8,128)S(1)}) %tuple.57, (pred[112,1024]{1,0:T(8,128)(4,1)S(1)}, ...), branch_computations={%region_4.4_spmd, %region_5.7_spmd} | conditional | flops 963841536 | bytes 28967968 | solution.py:66
  903.9 3.0 fusion.2
  907.0 2.4 fusion.4
  909.4 3.9 fusion.13
  913.3 0.7 dynamic_slice.40
  914.7 0.7 iota_compare_fusion.3
  915.5 0.9 fusion.27
  917.1 9.4 %conditional.3 = ((f32[8,2,112]{2,1,0:T(2,128)S(1)}, f32[8,2,112]{2,1,0:T(2,128)S(1)}, f32[8,2,112,128]{3,2,1,0:T(8,128)S(1)})) conditional(s32[]{:T(128)} %convert_element_type.39, (f32[8,2,112]{2,1,0:T(2,128)S(1)}, f32[8,2,112]{2,1,0:T(2,128)S(1)}, f32[8,2,112,128]{3,2,1,0:T(8,128)S(1)}) %tuple.57, (pred[112,1024]{1,0:T(8,128)(4,1)S(1)}, ...), branch_computations={%region_4.4_spmd, %region_5.7_spmd} | conditional | flops 963841536 | bytes 28967968 | solution.py:66
  917.1 3.0 fusion.2
  920.2 2.4 fusion.4
  922.6 3.9 fusion.13
  926.5 0.3 fusion.23
  926.8 0.4 copy.14
  927.2 1.1 convert_element_type.29
  (76 shorter events, 1.2 us)
Async XLA Ops:
  6.5 407.8 %all-gather.3.cloned.1.call-start = ((), (), s32[]{:S(2)}) async-start(), calls=%async_computation | async-start | bytes 14909440 | tf_op jit(solution)/shard_map/all_gather | solution.py:69
  7.3 811.3 %all-gather.5.cloned.1.call-start = ((), (), s32[]{:S(2)}) async-start(), calls=%async_computation.1 | async-start | bytes 14909440 | tf_op jit(solution)/shard_map/all_gather | solution.py:70
  827.7 6.5 copy-start
Sparse Core Ops, SparseCore 0:
  9.1 405.1 all-gather.2
  416.1 402.4 all-gather.4
where the time goes:
time: 936 us; the launch traced here: 935 us
  waiting for transfers between devices  793 us (85%)
  matrix products  48.3 us (5%)
  local copies, waits for them, and re-layouts  38.8 us (4%)
  other arithmetic  30.4 us (3%)
  between operations  14.2 us (2%)
  loops' own time  10.6 us (1%)
    all_gather x1, waiting for transfers between devices, shards(): key_piece = lax.all_gather(key_rows, 'ctx', axis=1, tiled=True)  403 us
    all_gather x1, waiting for transfers between devices, shards(): value_piece = lax.all_gather(value_rows, 'ctx', axis=1, tiled=True)  389 us
    unnamed x7, local copies, waits for them, and re-layouts  31.3 us
    dot_general x7, matrix products, update(): jnp.einsum('kgqs,skd->kgqd', weights.astype(jnp.bfloat16), value_block, p...  27.2 us
    dot_general x7, matrix products, update(): jnp.einsum('qkgd,skd->kgqs', query_heads, key_block, preferred_element_ty...  21.2 us
  transfers between devices with their start and end apart: 2, of which 2 were waited for; matrix products, arithmetic and copies ran while one was open for 2% of the time, Pallas kernels for 0%

commit v1 on v0

--- a/solution.py
+++ b/solution.py
@@ -66,7 +66,10 @@
         return lax.cond(jnp.any(visible), update, lambda carried: carried, state)
 
     start = jnp.int32(0)
-    key_piece = lax.all_gather(key_rows, "ctx", axis=1, tiled=True)
+    devices = lax.axis_size("ctx")
+    tiles = jnp.stack([key_rows for _ in range(devices)])
+    tiles = lax.all_to_all(tiles, "ctx", split_axis=0, concat_axis=0)
+    key_piece = jnp.concatenate(tiles, axis=1)
     value_piece = lax.all_gather(value_rows, "ctx", axis=1, tiled=True)
     piece_rows = key_piece.shape[1]
     block_rows = max(

time: 936 us -> 794 us (0.85)
  waiting for transfers between devices: 793 us -> 634 us
  starting transfers between devices: 0.04 us -> 11 us
    all_to_all x0 -> x1, waiting for transfers between devices: none -> 569 us  [shards(): tiles = lax.all_to_all(tiles, 'ctx', split_axis=0, concat_axis=0)]
    all_gather x1 -> x0, waiting for transfers between devices: 403 us -> none  [shards(): key_piece = lax.all_gather(key_rows, 'ctx', axis=1, tiled=True)]
    all_gather x1, waiting for transfers between devices: 389 us -> 63.8 us  [shards(): value_piece = lax.all_gather(value_rows, 'ctx', axis=1, tiled=True)]
    all_to_all x0 -> x1, starting transfers between devices: none -> 10.9 us  [shards(): tiles = lax.all_to_all(tiles, 'ctx', split_axis=0, concat_axis=0)]
    unnamed x7 -> x9, local copies, waits for them, and re-layouts: 31.3 us -> 31.3 us
where the time goes in v1:
time: 794 us; the launch traced here: 791 us
  waiting for transfers between devices  634 us (80%)
  matrix products  48.4 us (6%)
  local copies, waits for them, and re-layouts  45.5 us (6%)
  other arithmetic  28.8 us (4%)
  between operations  14.2 us (2%)
  starting transfers between devices  11 us (1%)
  loops' own time  9.45 us (1%)
    all_to_all x1, waiting for transfers between devices, shards(): tiles = lax.all_to_all(tiles, 'ctx', split_axis=0, concat_axis=0)  569 us
    all_gather x1, waiting for transfers between devices, shards(): value_piece = lax.all_gather(value_rows, 'ctx', axis=1, tiled=True)  63.8 us
    unnamed x9, local copies, waits for them, and re-layouts  31.3 us
    dot_general x7, matrix products, update(): jnp.einsum('kgqs,skd->kgqd', weights.astype(jnp.bfloat16), value_block, p...  27.2 us
    dot_general x7, matrix products, update(): jnp.einsum('qkgd,skd->kgqs', query_heads, key_block, preferred_element_ty...  21.2 us
    reduce_sum x7, other arithmetic, update(): new_total = running_total * factor + jnp.sum(weights, axis=-1)  16.7 us
  transfers between devices with their start and end apart: 2, of which 2 were waited for; matrix products, arithmetic and copies ran while one was open for 2% of the time, Pallas kernels for 0%

profile of v1, /device:TPU:126, one launch (start us, length us, event | category | flops | bytes accessed | tf_op | source)
XLA Modules:
  0.0 791.1 jit_solution(5427171546747754660)
XLA Ops:
  6.5 8.0 %stack.2 = bf16[64,1,112,1024]{3,2,1,0:T(8,128)(2,1)} broadcast(bf16[112,1024]{1,0:T(8,128)(2,1)} %bitcast.68), dimensions={2,3} | broadcast | bytes 14909440 | tf_op jit(solution)/shard_map/stack | solution.py:70
  14.6 10.9 %all-to-all-start = ((bf16[64,1,112,1024]{3,2,1,0:T(8,128)(2,1)}), bf16[64,1,112,1024]{3,2,1,0:T(8,128)(2,1)}, u32[]{:S(2)}, u32[]{:S(2)}) async-start(bf16[64,1,112,1024]{3,2,1,0:T(8,128)(2,1)} %stack.2), calls=%async_computation | async-start | bytes 29360128 | tf_op jit(solution)/shard_map/all_to_all | solution.py:71
  25.6 0.7 all-gather.2.cloned.1.call-update
  26.9 0.3 reshape_squeeze.6
  27.2 0.1 copy.16
  27.5 569.3 %all-to-all-done = bf16[64,1,112,1024]{3,2,1,0:T(8,128)(2,1)} async-done(((bf16[64,1,112,1024]{3,2,1,0:T(8,128)(2,1)}), bf16[64,1,112,1024]{3,2,1,0:T(8,128)(2,1)}, u32[]{:S(2)}, u32[]{:S(2)}) %all-to-all-start) | async-done | bytes 14680096 | tf_op jit(solution)/shard_map/all_to_all | solution.py:71
  596.8 9.1 %copy.21 = bf16[896,8,8,128]{3,2,1,0:T(8,128)(2,1)S(1)} copy(bf16[896,8,8,128]{3,1,2,0:T(8,128)(2,1)} %bitcast.18) | data formatting | bytes 29360128
  606.0 6.5 copy.15
  612.5 63.8 %all-gather.2.cloned.1.call-done = bf16[1,7168,1024]{2,1,0:T(8,128)(2,1)} async-done(((bf16[1,112,1024]{2,1,0:T(8,128)(2,1)}), bf16[1,7168,1024]{2,1,0:T(8,128)(2,1)}) %all-gather.2.cloned.1.call-update) | async-done | bytes 14680080 | tf_op jit(solution)/shard_map/all_gather | solution.py:73
  676.3 9.1 %copy.22 = bf16[896,8,8,128]{3,2,1,0:T(8,128)(2,1)S(1)} copy(bf16[896,8,8,128]{3,1,2,0:T(8,128)(2,1)} %bitcast.62) | data formatting | bytes 29360128
  685.5 6.4 copy.17
  692.0 90.5 %while.17 = (s32[]{:T(128)}, f32[8,2,112]{2,1,0:T(2,128)S(1)}, f32[8,2,112]{2,1,0:T(2,128)S(1)}, f32[8,2,112,128]{3,2,1,0:T(8,128)S(1)}, s32[7]{0:T(128)S(1)}, /...) while((s32[]{:T(128)}, f32[8,2,112]{2,1,0:T(2,128)S(1)}, ...), condition=%wide.region_8.9_spmd.clone, body=%wide.region_1.8_spmd.clone.sunk | while | flops 964502272 | bytes 29113972 | solution.py:87
  692.0 0.6 dynamic_slice.40
  693.2 0.7 iota_compare_fusion.3
  694.0 0.9 fusion.27
  695.5 9.4 %conditional.3 = ((f32[8,2,112]{2,1,0:T(2,128)S(1)}, f32[8,2,112]{2,1,0:T(2,128)S(1)}, f32[8,2,112,128]{3,2,1,0:T(8,128)S(1)})) conditional(s32[]{:T(128)} %convert_element_type.39, (f32[8,2,112]{2,1,0:T(2,128)S(1)}, f32[8,2,112]{2,1,0:T(2,128)S(1)}, f32[8,2,112,128]{3,2,1,0:T(8,128)S(1)}) %tuple.58, (pred[112,1024]{1,0:T(8,128)(4,1)S(1)}, ...), branch_computations={%region_4.4_spmd, %region_5.7_spmd} | conditional | flops 963841536 | bytes 28967968 | solution.py:66
  695.5 3.0 fusion.2
  698.6 2.4 fusion.4
  701.0 3.9 fusion.13
  704.9 0.6 dynamic_slice.40
  706.2 0.7 iota_compare_fusion.3
  707.0 0.9 fusion.27
  708.4 9.4 %conditional.3 = ((f32[8,2,112]{2,1,0:T(2,128)S(1)}, f32[8,2,112]{2,1,0:T(2,128)S(1)}, f32[8,2,112,128]{3,2,1,0:T(8,128)S(1)})) conditional(s32[]{:T(128)} %convert_element_type.39, (f32[8,2,112]{2,1,0:T(2,128)S(1)}, f32[8,2,112]{2,1,0:T(2,128)S(1)}, f32[8,2,112,128]{3,2,1,0:T(8,128)S(1)}) %tuple.58, (pred[112,1024]{1,0:T(8,128)(4,1)S(1)}, ...), branch_computations={%region_4.4_spmd, %region_5.7_spmd} | conditional | flops 963841536 | bytes 28967968 | solution.py:66
  708.5 3.0 fusion.2
  711.5 2.4 fusion.4
  713.9 3.9 fusion.13
  717.8 0.6 dynamic_slice.40
  719.1 0.7 iota_compare_fusion.3
  719.9 0.9 fusion.27
  721.4 9.4 %conditional.3 = ((f32[8,2,112]{2,1,0:T(2,128)S(1)}, f32[8,2,112]{2,1,0:T(2,128)S(1)}, f32[8,2,112,128]{3,2,1,0:T(8,128)S(1)})) conditional(s32[]{:T(128)} %convert_element_type.39, (f32[8,2,112]{2,1,0:T(2,128)S(1)}, f32[8,2,112]{2,1,0:T(2,128)S(1)}, f32[8,2,112,128]{3,2,1,0:T(8,128)S(1)}) %tuple.58, (pred[112,1024]{1,0:T(8,128)(4,1)S(1)}, ...), branch_computations={%region_4.4_spmd, %region_5.7_spmd} | conditional | flops 963841536 | bytes 28967968 | solution.py:66
  721.4 3.0 fusion.2
  724.4 2.4 fusion.4
  726.8 3.9 fusion.13
  730.8 0.6 dynamic_slice.40
  732.0 0.7 iota_compare_fusion.3
  732.8 0.9 fusion.27
  734.3 9.4 %conditional.3 = ((f32[8,2,112]{2,1,0:T(2,128)S(1)}, f32[8,2,112]{2,1,0:T(2,128)S(1)}, f32[8,2,112,128]{3,2,1,0:T(8,128)S(1)})) conditional(s32[]{:T(128)} %convert_element_type.39, (f32[8,2,112]{2,1,0:T(2,128)S(1)}, f32[8,2,112]{2,1,0:T(2,128)S(1)}, f32[8,2,112,128]{3,2,1,0:T(8,128)S(1)}) %tuple.58, (pred[112,1024]{1,0:T(8,128)(4,1)S(1)}, ...), branch_computations={%region_4.4_spmd, %region_5.7_spmd} | conditional | flops 963841536 | bytes 28967968 | solution.py:66
  734.3 3.0 fusion.2
  737.4 2.4 fusion.4
  739.8 3.9 fusion.13
  743.7 0.6 dynamic_slice.40
  744.9 0.7 iota_compare_fusion.3
  745.7 0.9 fusion.27
  747.2 9.4 %conditional.3 = ((f32[8,2,112]{2,1,0:T(2,128)S(1)}, f32[8,2,112]{2,1,0:T(2,128)S(1)}, f32[8,2,112,128]{3,2,1,0:T(8,128)S(1)})) conditional(s32[]{:T(128)} %convert_element_type.39, (f32[8,2,112]{2,1,0:T(2,128)S(1)}, f32[8,2,112]{2,1,0:T(2,128)S(1)}, f32[8,2,112,128]{3,2,1,0:T(8,128)S(1)}) %tuple.58, (pred[112,1024]{1,0:T(8,128)(4,1)S(1)}, ...), branch_computations={%region_4.4_spmd, %region_5.7_spmd} | conditional | flops 963841536 | bytes 28967968 | solution.py:66
  747.2 3.0 fusion.2
  750.3 2.4 fusion.4
  752.7 3.9 fusion.13
  756.6 0.6 dynamic_slice.40
  757.9 0.7 iota_compare_fusion.3
  758.7 0.9 fusion.27
  760.1 9.4 %conditional.3 = ((f32[8,2,112]{2,1,0:T(2,128)S(1)}, f32[8,2,112]{2,1,0:T(2,128)S(1)}, f32[8,2,112,128]{3,2,1,0:T(8,128)S(1)})) conditional(s32[]{:T(128)} %convert_element_type.39, (f32[8,2,112]{2,1,0:T(2,128)S(1)}, f32[8,2,112]{2,1,0:T(2,128)S(1)}, f32[8,2,112,128]{3,2,1,0:T(8,128)S(1)}) %tuple.58, (pred[112,1024]{1,0:T(8,128)(4,1)S(1)}, ...), branch_computations={%region_4.4_spmd, %region_5.7_spmd} | conditional | flops 963841536 | bytes 28967968 | solution.py:66
  760.2 3.0 fusion.2
  763.2 2.4 fusion.4
  765.6 3.9 fusion.13
  769.5 0.6 dynamic_slice.40
  770.8 0.7 iota_compare_fusion.3
  771.6 0.9 fusion.27
  773.1 9.4 %conditional.3 = ((f32[8,2,112]{2,1,0:T(2,128)S(1)}, f32[8,2,112]{2,1,0:T(2,128)S(1)}, f32[8,2,112,128]{3,2,1,0:T(8,128)S(1)})) conditional(s32[]{:T(128)} %convert_element_type.39, (f32[8,2,112]{2,1,0:T(2,128)S(1)}, f32[8,2,112]{2,1,0:T(2,128)S(1)}, f32[8,2,112,128]{3,2,1,0:T(8,128)S(1)}) %tuple.58, (pred[112,1024]{1,0:T(8,128)(4,1)S(1)}, ...), branch_computations={%region_4.4_spmd, %region_5.7_spmd} | conditional | flops 963841536 | bytes 28967968 | solution.py:66
  773.1 3.0 fusion.2
  776.1 2.4 fusion.4
  778.5 3.9 fusion.13
  782.5 0.3 fusion.23
  782.8 0.4 copy.18
  783.1 1.1 convert_element_type.29
  (78 shorter events, 1.2 us)
Async XLA Ops:
  14.6 12.3 %copy-start = (bf16[1,112,2048]{2,1,0:T(8,128)(2,1)S(1)}, bf16[1,112,2048]{2,1,0:T(8,128)(2,1)}, u32[]{:S(2)}) copy-start(bf16[1,112,2048]{2,1,0:T(8,128)(2,1)} %param.9) | copy-start | bytes 1376260
  14.6 12.8 %copy-start.1 = (s32[1,14]{1,0:T(1,128)S(1)}, s32[1,14]{1,0:T(1,128)}, u32[]{:S(2)}) copy-start(s32[1,14]{1,0:T(1,128)} %param.12) | copy-start | bytes 172
  14.6 582.3 %all-to-all-start = ((bf16[64,1,112,1024]{3,2,1,0:T(8,128)(2,1)}), bf16[64,1,112,1024]{3,2,1,0:T(8,128)(2,1)}, u32[]{:S(2)}, u32[]{:S(2)}) async-start(bf16[64,1,112,1024]{3,2,1,0:T(8,128)(2,1)} %stack.2), calls=%async_computation | async-start | bytes 29360128 | tf_op jit(solution)/shard_map/all_to_all | solution.py:71
  25.5 650.8 %all-gather.2.cloned.1.call-start = ((), (), s32[]{:S(2)}) async-start(), calls=%async_computation.1 | async-start | bytes 14909440 | tf_op jit(solution)/shard_map/all_gather | solution.py:73
Sparse Core Ops, SparseCore 0:
  28.1 648.1 all-gather.1
